TPU v7x, 32 devices: a whole 2x2x4 slice. The times are simulated.
32 devices in a mesh: tm: 8 (over z, y), head: 4 (over x, core).
Axes of the slice: x: 2, y: 2, z: 4, core: 2. Of those that a mesh axis runs over, the one named last changes fastest.
Arguments:
- queries: bfloat16 [6144, 1536], P('tm', 'head'), may hold values from -6 to 6
- key_rows: bfloat16 [6144, 1536], P('tm', 'head'), may hold values from -6 to 6
- value_rows: bfloat16 [6144, 1536], P('tm', 'head'), may hold values from -6 to 6
- grad_out: bfloat16 [6144, 3072], P('tm', 'head'), may hold values from -192 to 192
- w_out: bfloat16 [1536, 3072], P('head', 'tm'), may hold values from -0.109375 to 0.109375
Outputs:
- grad_queries: bfloat16 [6144, 1536], P('tm', 'head')
- grad_keys: bfloat16 [6144, 1536], P('tm', 'head')
- grad_values: bfloat16 [6144, 1536], P('tm', 'head')
All inputs are finite; a program needn't handle non-finite values.
Results may differ from a plain program's by a relative error of at most 0.0081.
Values may be sent and summed in bfloat16 or wider, within the bound.
No kernel may reach another device: no remote copies, remote signals or barrier semaphores. Data moves between devices by JAX's collectives and lax.ppermute only.
A program may use at most 128 MiB of HBM per device.

v0:
```python
import math
import jax
import jax.numpy as jnp
from jax import lax
from jax.sharding import PartitionSpec as P

HD = 128
TILE_T = 6
TILE_H = 8
TILE_W = 8
VT = 8


def passed_along(block, axis, distance):
    devices = range(lax.axis_size(axis))
    route = [(i - distance, i) for i in devices if i - distance in devices]
    return lax.ppermute(block, axis, route)


def tile_range(index, count):
    return (max(index - 1, 0), min(index + 1, count - 1))


def local(queries, key_rows, value_rows, grad_out, w_out):
    token_count, local_width = queries.shape
    head_count = local_width // HD
    tile_size = TILE_T * TILE_H * TILE_W
    tile_count = token_count // tile_size
    inverse_root = 1.0 / math.sqrt(HD)
    video_place = lax.axis_index("tm") % VT
    flags = (video_place > 0, video_place >= 0, video_place < VT - 1)
    full_grad = lax.all_gather(grad_out, "head", axis=1, tiled=True)
    attn_sum = jnp.einsum(
        "td,hd->th",
        full_grad,
        lax.all_gather(w_out, "tm", axis=1, tiled=True),
        preferred_element_type=jnp.float32,
    )
    attn_grad = attn_sum.astype(jnp.bfloat16)
    before_keys, before_values = passed_along((key_rows, value_rows), "tm", 1)
    after_keys, after_values = passed_along((key_rows, value_rows), "tm", -1)
    slab_keys = (before_keys, key_rows, after_keys)
    slab_values = (before_values, value_rows, after_values)
    zero_tile = jnp.zeros((tile_size, local_width), jnp.float32)
    key_sums = [[zero_tile] * tile_count for other in range(3)]
    value_sums = [[zero_tile] * tile_count for other in range(3)]
    query_grads = []
    for tile_index in range(tile_count):
        lower, upper = tile_range(tile_index, tile_count)
        width_rows = (upper - lower + 1) * tile_size
        key_block = jnp.concatenate([part for part in slab_keys], 0)
        key_block = key_block.reshape(3 * width_rows, head_count, HD)
        value_block = jnp.concatenate([part for part in slab_values], 0)
        value_block = value_block.reshape(3 * width_rows, head_count, HD)
        key_mask = jnp.concatenate([jnp.broadcast_to(flag, (width_rows,)) for flag in flags], 0)
        query_tile = queries[tile_index * tile_size : (tile_index + 1) * tile_size].reshape(
            tile_size, head_count, HD
        )
        grad_tile = attn_grad[tile_index * tile_size : (tile_index + 1) * tile_size].reshape(
            tile_size, head_count, HD
        )
        scores = (
            jnp.einsum("qhd,khd->hqk", query_tile, key_block, preferred_element_type=jnp.float32)
            * inverse_root
        )
        scores = jnp.where(key_mask[None, None, :], scores, -jnp.inf)
        row_peak = jnp.max(scores, axis=2, keepdims=True)
        weights = jnp.exp(scores - row_peak)
        row_total = jnp.sum(weights, axis=2, keepdims=True)
        softmax_rows = weights / row_total
        softmax_grad = jnp.einsum(
            "qhd,khd->hqk", grad_tile, value_block, preferred_element_type=jnp.float32
        )
        row_inner = jnp.sum(softmax_rows * softmax_grad, axis=2, keepdims=True)
        score_grad = (softmax_rows * (softmax_grad - row_inner)).astype(jnp.bfloat16)
        softmax_low = softmax_rows.astype(jnp.bfloat16)
        grad_query = (
            jnp.einsum("hqk,khd->qhd", score_grad, key_block, preferred_element_type=jnp.float32)
            * inverse_root
        )
        query_grads.append(grad_query.reshape(tile_size, local_width).astype(jnp.bfloat16))
        kept = (0, 1, 2)
        key_part = (
            jnp.einsum("hqk,qhd->khd", score_grad, query_tile, preferred_element_type=jnp.float32)
            * inverse_root
        )
        key_part = key_part.reshape(len(kept) * width_rows, local_width)
        value_part = jnp.einsum(
            "hqk,qhd->khd", softmax_low, grad_tile, preferred_element_type=jnp.float32
        )
        value_part = value_part.reshape(len(kept) * width_rows, local_width)
        for position, slab_index in enumerate(kept):
            for neighbour in range(lower, upper + 1):
                offset = position * width_rows + (neighbour - lower) * tile_size
                key_sums[slab_index][neighbour] = (
                    key_sums[slab_index][neighbour] + key_part[offset : offset + tile_size]
                )
                value_sums[slab_index][neighbour] = (
                    value_sums[slab_index][neighbour] + value_part[offset : offset + tile_size]
                )
    own_keys = jnp.concatenate(key_sums[1], 0)
    own_values = jnp.concatenate(value_sums[1], 0)
    later_keys, later_values = (
        passed_along(jnp.concatenate(key_sums[0], 0).astype(jnp.bfloat16), "tm", -1).astype(
            jnp.float32
        ),
        passed_along(jnp.concatenate(value_sums[0], 0).astype(jnp.bfloat16), "tm", -1).astype(
            jnp.float32
        ),
    )
    earlier_keys, earlier_values = (
        passed_along(jnp.concatenate(key_sums[2], 0).astype(jnp.bfloat16), "tm", 1).astype(
            jnp.float32
        ),
        passed_along(jnp.concatenate(value_sums[2], 0).astype(jnp.bfloat16), "tm", 1).astype(
            jnp.float32
        ),
    )
    grad_keys = own_keys + later_keys + earlier_keys
    grad_values = own_values + later_values + earlier_values
    grad_queries = jnp.concatenate(query_grads, 0)
    return (grad_queries, grad_keys.astype(jnp.bfloat16), grad_values.astype(jnp.bfloat16))


def solution(mesh):
    placed = (P("tm", "head"), P("tm", "head"), P("tm", "head"), P("tm", "head"), P("head", "tm"))
    return jax.shard_map(
        local,
        mesh=mesh,
        in_specs=placed,
        out_specs=(P("tm", "head"), P("tm", "head"), P("tm", "head")),
        check_vma=False,
    )
```

profile of v0, /device:TPU:0, one launch (start us, length us, event | category | flops | bytes accessed | tf_op | source)
XLA Modules:
  0.0 249.1 jit_solution(441162464719006397)
XLA Ops:
  11.3 6.4 %collective-permute-start.2 = (bf16[768,384]{0,1:T(8,128)(2,1)S(1)}, bf16[768,384]{0,1:T(8,128)(2,1)}, u32[]{:S(2)}, u32[]{:S(2)}) collective-permute-start(bf16[768,384]{0,1:T(8,128)(2,1)S(1)} %copy.44), channel_id=1, source_target_pairs={{0,4},{4,8},{8,12},{12,16},{16,20},{20,24},{24,28},{1,5},{5,9},{9,... | collective-permute-start | bytes 1769480 | tf_op jit(solution)/shard_map/ppermute | solution.py:17
  20.2 5.4 %collective-permute-start = (bf16[768,384]{0,1:T(8,128)(2,1)S(1)}, bf16[768,384]{0,1:T(8,128)(2,1)}, u32[]{:S(2)}, u32[]{:S(2)}) collective-permute-start(bf16[768,384]{0,1:T(8,128)(2,1)S(1)} %copy.38), channel_id=1, source_target_pairs={{0,4},{4,8},{8,12},{12,16},{16,20},{20,24},{24,28},{1,5},{5,9},{9,... | collective-permute-start | bytes 1769480 | tf_op jit(solution)/shard_map/ppermute | solution.py:17
  26.3 5.9 %collective-permute-done.3 = bf16[768,384]{0,1:T(8,128)(2,1)S(1)} collective-permute-done((bf16[768,384]{0,1:T(8,128)(2,1)S(1)}, bf16[768,384]{0,1:T(8,128)(2,1)S(1)}, u32[]{:S(2)}, u32[]{:S(2)}) %collective-permute-start.3) | collective-permute-done | bytes 589856 | tf_op jit(solution)/shard_map/ppermute | solution.py:17
  32.2 24.7 %collective-permute-done.2 = bf16[768,384]{0,1:T(8,128)(2,1)} collective-permute-done((bf16[768,384]{0,1:T(8,128)(2,1)S(1)}, bf16[768,384]{0,1:T(8,128)(2,1)}, u32[]{:S(2)}, u32[]{:S(2)}) %collective-permute-start.2) | collective-permute-done | bytes 589856 | tf_op jit(solution)/shard_map/ppermute | solution.py:17
  56.9 2.5 pad_maximum_fusion.1
  60.2 11.8 %collective-permute-done = bf16[768,384]{0,1:T(8,128)(2,1)} collective-permute-done((bf16[768,384]{0,1:T(8,128)(2,1)S(1)}, bf16[768,384]{0,1:T(8,128)(2,1)}, u32[]{:S(2)}, u32[]{:S(2)}) %collective-permute-start) | collective-permute-done | bytes 589856 | tf_op jit(solution)/shard_map/ppermute | solution.py:17
  73.4 7.7 %fusion.52 = (f32[3,384]{1,0:T(4,128)S(1)}, f32[3,384,2304]{1,2,0:T(8,128)}) fusion(pred[2304]{0:T(1024)(128)(4,1)S(1)} %pad_add_fusion, bf16[2304,3,128]{0,2,1:T(8,128)(2,1)S(1)} %bitcast.78, bf16[384,3,128]{0,2,1:T(8,128)(2,1)S(1)} %bitcast.95), kind=kOutput, calls=%fused_computation.81 | convolution fusion | flops 690096384 | bytes 12688128 | tf_op jit(solution)/shard_map/sub | solution.py:68
  81.0 7.8 %fusion.53 = (f32[3,384]{1,0:T(4,128)S(1)}, f32[3,384,2304]{1,2,0:T(8,128)}) fusion(pred[2304]{0:T(1024)(128)(4,1)S(1)} %pad_add_fusion, bf16[2304,3,128]{0,2,1:T(8,128)(2,1)S(1)} %bitcast.79, bf16[384,3,128]{0,2,1:T(8,128)(2,1)S(1)} %bitcast.92), kind=kOutput, calls=%fused_computation.82 | convolution fusion | flops 690096384 | bytes 12688128 | tf_op jit(solution)/shard_map/sub | solution.py:68
  88.9 3.6 %all-gather.5.cloned.1.call-done = bf16[384,3072]{1,0:T(8,128)(2,1)} async-done(((bf16[384,384]{1,0:T(8,128)(2,1)}), bf16[384,3072]{1,0:T(8,128)(2,1)}) %all-gather.5.cloned.1.call-update) | async-done | bytes 2359312 | tf_op jit(solution)/shard_map/all_gather | solution.py:36
  92.5 39.1 %all-gather.3.cloned.1.call-done = bf16[768,3072]{1,0:T(8,128)(2,1)} async-done(((bf16[768,768]{1,0:T(8,128)(2,1)}), bf16[768,3072]{1,0:T(8,128)(2,1)}) %all-gather.3.cloned.1.call-update) | async-done | bytes 4718608 | tf_op jit(solution)/shard_map/all_gather | solution.py:32
  131.6 5.1 %convolution_convert_fusion = bf16[768,384]{0,1:T(8,128)(2,1)S(1)} fusion(bf16[768,3072]{1,0:T(8,128)(2,1)} %all-gather.3.cloned.1.call-done, bf16[384,3072]{1,0:T(8,128)(2,1)} %all-gather.5.cloned.1.call-done), kind=kOutput, calls=%fused_computation.36 | convolution fusion | flops 1812234240 | bytes 7667712 | tf_op jit(solution)/shard_map/td,hd->th/dot_general | solution.py:33
  136.8 5.8 %fusion.25 = f32[2304,3,128]{0,2,1:T(8,128)S(1)} fusion(bf16[384,3,128]{0,2,1:T(8,128)(2,1)S(1)} %bitcast.108, f32[3,384,2304]{1,2,0:T(8,128)} %get-tuple-element.20, f32[3,384]{1,0:T(4,128)S(1)} %get-tuple-element.19), kind=kOutput, calls=%fused_computation.33 | convolution fusion | flops 684785664 | bytes 14455296 | tf_op jit(solution)/shard_map/hqk,qhd->khd/dot_general | solution.py:88
  144.3 5.0 %multiply_reduce_fusion = (f32[3,384]{1,0:T(4,128)S(1)}, f32[3,384,2304]{1,2,0:T(8,128)}) fusion(f32[3,384,2304]{1,2,0:T(8,128)S(1)} %bitcast.85, f32[3,384]{1,0:T(4,128)S(1)} %get-tuple-element.19, bf16[384,3,128]{0,2,1:T(8,128)(2,1)S(1)} %bitcast.109, bf16[2304,3,128]{0,2,1:T(8,128)(2,1)S(1)} %bitcast.90), kind=kOutput, calls=%fused_computation.11 | convolution fusion | flops 687438720 | bytes 23307264 | tf_op jit(solution)/shard_map/qhd,khd->hqk/dot_general | solution.py:71
  149.4 8.3 %multiply_convert_fusion = bf16[3,384,2304]{1,2,0:T(8,128)(2,1)S(1)} fusion(f32[3,384,2304]{1,2,0:T(8,128)} %get-tuple-element.22, f32[3,384]{1,0:T(4,128)S(1)} %get-tuple-element.21, f32[3,384,2304]{1,2,0:T(8,128)} %get-tuple-element.20, f32[3,384]{1,0:T(4,128)S(1)} %get-tuple-element.19), kind=kLoop, calls=%fused_computation.10 | loop fusion | flops 10616832 | bytes 26551296 | tf_op jit(solution)/shard_map/convert_element_type | solution.py:75
  159.5 3.4 %fusion.21 = f32[2304,3,128]{0,2,1:T(8,128)} fusion(bf16[3,384,2304]{1,2,0:T(8,128)(2,1)S(1)} %multiply_convert_fusion, bf16[384,3,128]{0,2,1:T(8,128)(2,1)S(1)} %bitcast.96), kind=kOutput, calls=%fused_computation.31 | convolution fusion | flops 680361984 | bytes 9142272 | tf_op jit(solution)/shard_map/hqk,qhd->khd/dot_general | solution.py:84
  164.5 5.0 %multiply_reduce_fusion.1 = (f32[3,384]{1,0:T(4,128)S(1)}, f32[3,384,2304]{1,2,0:T(8,128)}) fusion(f32[3,384,2304]{1,2,0:T(8,128)S(1)} %bitcast.83, f32[3,384]{1,0:T(4,128)S(1)} %get-tuple-element.23, bf16[384,3,128]{0,2,1:T(8,128)(2,1)S(1)} %bitcast.107, bf16[2304,3,128]{0,2,1:T(8,128)(2,1)S(1)} %bitcast.91), kind=kOutput, calls=%fused_computation.14 | convolution fusion | flops 687438720 | bytes 23307264 | tf_op jit(solution)/shard_map/qhd,khd->hqk/dot_general | solution.py:71
  170.7 1.9 copy.74
  177.2 2.0 pad_maximum_fusion.5
  180.5 1.9 pad_maximum_fusion.6
  182.4 5.4 %collective-permute-start.7 = (bf16[768,384]{1,0:T(8,128)(2,1)}, bf16[768,384]{1,0:T(8,128)(2,1)}, u32[]{:S(2)}, u32[]{:S(2)}) collective-permute-start(bf16[768,384]{1,0:T(8,128)(2,1)} %pad_maximum_fusion.6), channel_id=1, source_target_pairs={{0,4},{4,8},{8,12},{12,16},{16,20},{20,24},{24,28},{1,5},{5,9},{9,... | collective-permute-start | bytes 1769480 | tf_op jit(solution)/shard_map/ppermute | solution.py:17
  187.7 7.9 %multiply_convert_fusion.1 = bf16[3,384,2304]{1,2,0:T(8,128)(2,1)S(1)} fusion(f32[3,384,2304]{1,2,0:T(8,128)} %get-tuple-element.26, f32[3,384]{1,0:T(4,128)S(1)} %get-tuple-element.25, f32[3,384,2304]{1,2,0:T(8,128)} %get-tuple-element.24, f32[3,384]{1,0:T(4,128)S(1)} %get-tuple-element.23), kind=kLoop, calls=%fused_computation.13 | loop fusion | flops 10616832 | bytes 26551296 | tf_op jit(solution)/shard_map/convert_element_type | solution.py:75
  201.0 1.9 copy.66
  202.8 1.9 copy.69
  204.7 1.9 copy.68
  208.4 1.9 pad_maximum_fusion.3
  211.6 1.9 pad_maximum_fusion.4
  213.5 5.4 %collective-permute-start.5 = (bf16[768,384]{1,0:T(8,128)(2,1)}, bf16[768,384]{1,0:T(8,128)(2,1)}, u32[]{:S(2)}, u32[]{:S(2)}) collective-permute-start(bf16[768,384]{1,0:T(8,128)(2,1)} %pad_maximum_fusion.4), channel_id=1, source_target_pairs={{0,4},{4,8},{8,12},{12,16},{16,20},{20,24},{24,28},{1,5},{5,9},{9,... | collective-permute-start | bytes 1769480 | tf_op jit(solution)/shard_map/ppermute | solution.py:17
  218.9 4.3 %fusion.28 = bf16[3,128,384]{2,1,0:T(8,128)(2,1)} fusion(bf16[2304,3,128]{0,2,1:T(8,128)(2,1)S(1)} %bitcast.81, bf16[3,384,2304]{1,2,0:T(8,128)(2,1)} %copy-done), kind=kOutput, calls=%fused_computation.39 | convolution fusion | flops 679772160 | bytes 7372800 | tf_op jit(solution)/shard_map/hqk,khd->qhd/dot_general | solution.py:78
  223.2 1.9 copy.61
  229.1 2.2 fusion.33
  231.4 8.7 %collective-permute-done.5 = bf16[768,384]{1,0:T(8,128)(2,1)} collective-permute-done((bf16[768,384]{1,0:T(8,128)(2,1)}, bf16[768,384]{1,0:T(8,128)(2,1)}, u32[]{:S(2)}, u32[]{:S(2)}) %collective-permute-start.5) | collective-permute-done | bytes 589856 | tf_op jit(solution)/shard_map/ppermute | solution.py:17
  240.0 2.2 fusion.31
  (64 shorter events, 34.0 us)
Async XLA Ops:
  7.2 18.5 %copy-start.5 = (bf16[768,384]{1,0:T(8,128)(2,1)S(1)}, bf16[768,384]{1,0:T(8,128)(2,1)}, u32[]{:S(2)}) copy-start(bf16[768,384]{1,0:T(8,128)(2,1)} %param.5) | copy-start | bytes 1769476
  7.2 85.3 %all-gather.5.cloned.1.call-start = ((), (), s32[]{:S(2)}) async-start(), calls=%async_computation.1 | async-start | bytes 2654208 | tf_op jit(solution)/shard_map/all_gather | solution.py:36
  7.9 123.7 %all-gather.3.cloned.1.call-start = ((), (), s32[]{:S(2)}) async-start(), calls=%async_computation | async-start | bytes 5898240 | tf_op jit(solution)/shard_map/all_gather | solution.py:32
  10.0 22.2 %collective-permute-start.3 = (bf16[768,384]{0,1:T(8,128)(2,1)S(1)}, bf16[768,384]{0,1:T(8,128)(2,1)S(1)}, u32[]{:S(2)}, u32[]{:S(2)}) collective-permute-start(bf16[768,384]{0,1:T(8,128)(2,1)S(1)} %copy.44), channel_id=1, source_target_pairs={{4,0},{8,4},{12,8},{16,12},{20,16},{24,20},{28,24},{5,1},{9,5},{13... | collective-permute-start | bytes 1769480 | tf_op jit(solution)/shard_map/ppermute | solution.py:17
  11.3 45.6 %collective-permute-start.2 = (bf16[768,384]{0,1:T(8,128)(2,1)S(1)}, bf16[768,384]{0,1:T(8,128)(2,1)}, u32[]{:S(2)}, u32[]{:S(2)}) collective-permute-start(bf16[768,384]{0,1:T(8,128)(2,1)S(1)} %copy.44), channel_id=1, source_target_pairs={{0,4},{4,8},{8,12},{12,16},{16,20},{20,24},{24,28},{1,5},{5,9},{9,... | collective-permute-start | bytes 1769480 | tf_op jit(solution)/shard_map/ppermute | solution.py:17
  18.9 40.4 %collective-permute-start.1 = (bf16[768,384]{0,1:T(8,128)(2,1)S(1)}, bf16[768,384]{0,1:T(8,128)(2,1)S(1)}, u32[]{:S(2)}, u32[]{:S(2)}) collective-permute-start(bf16[768,384]{0,1:T(8,128)(2,1)S(1)} %copy.38), channel_id=1, source_target_pairs={{4,0},{8,4},{12,8},{16,12},{20,16},{24,20},{28,24},{5,1},{9,5},{13... | collective-permute-start | bytes 1769480 | tf_op jit(solution)/shard_map/ppermute | solution.py:17
  20.2 51.8 %collective-permute-start = (bf16[768,384]{0,1:T(8,128)(2,1)S(1)}, bf16[768,384]{0,1:T(8,128)(2,1)}, u32[]{:S(2)}, u32[]{:S(2)}) collective-permute-start(bf16[768,384]{0,1:T(8,128)(2,1)S(1)} %copy.38), channel_id=1, source_target_pairs={{0,4},{4,8},{8,12},{12,16},{16,20},{20,24},{24,28},{1,5},{5,9},{9,... | collective-permute-start | bytes 1769480 | tf_op jit(solution)/shard_map/ppermute | solution.py:17
  59.4 0.8 copy-start.4
  136.7 5.9 %slice-start.3 = ((s8[10616832]{0:T(1024)(128)(4,1)}), s8[4194304]{0:T(1024)(128)(4,1)S(1)}, s32[]{:S(2)}) async-start(s8[10616832]{0:T(1024)(128)(4,1)} %bitcast.84), calls=%async_computation.5 | async-start | bytes 8388608
  136.8 6.4 %slice-start.4 = ((s8[10616832]{0:T(1024)(128)(4,1)}), s8[4194304]{0:T(1024)(128)(4,1)S(1)}, s32[]{:S(2)}) async-start(s8[10616832]{0:T(1024)(128)(4,1)} %bitcast.84), calls=%async_computation.6 | async-start | bytes 8388608
  136.8 7.1 %slice-start.5 = ((s8[10616832]{0:T(1024)(128)(4,1)}), s8[2228224]{0:T(1024)(128)(4,1)S(1)}, s32[]{:S(2)}) async-start(s8[10616832]{0:T(1024)(128)(4,1)} %bitcast.84), calls=%async_computation.7 | async-start | bytes 4456448
  136.8 7.5 %copy-start.3 = (bf16[2304,384]{0,1:T(8,128)(2,1)S(1)}, bf16[2304,384]{0,1:T(8,128)(2,1)}, u32[]{:S(2)}) copy-start(bf16[2304,384]{0,1:T(8,128)(2,1)} %pad_maximum_fusion.1) | copy-start | bytes 5308420
  149.4 13.5 %slice-start = ((s8[10616832]{0:T(1024)(128)(4,1)}), s8[4194304]{0:T(1024)(128)(4,1)S(1)}, s32[]{:S(2)}) async-start(s8[10616832]{0:T(1024)(128)(4,1)} %bitcast.82), calls=%async_computation.2 | async-start | bytes 8388608
  149.4 13.5 %slice-start.1 = ((s8[10616832]{0:T(1024)(128)(4,1)}), s8[4194304]{0:T(1024)(128)(4,1)S(1)}, s32[]{:S(2)}) async-start(s8[10616832]{0:T(1024)(128)(4,1)} %bitcast.82), calls=%async_computation.3 | async-start | bytes 8388608
  157.7 5.2 %slice-start.2 = ((s8[10616832]{0:T(1024)(128)(4,1)}), s8[2228224]{0:T(1024)(128)(4,1)S(1)}, s32[]{:S(2)}) async-start(s8[10616832]{0:T(1024)(128)(4,1)} %bitcast.82), calls=%async_computation.4 | async-start | bytes 4456448
  179.2 49.9 %collective-permute-start.6 = (bf16[768,384]{1,0:T(8,128)(2,1)}, bf16[768,384]{1,0:T(8,128)(2,1)}, u32[]{:S(2)}, u32[]{:S(2)}) collective-permute-start(bf16[768,384]{1,0:T(8,128)(2,1)} %pad_maximum_fusion.5), channel_id=1, source_target_pairs={{4,0},{8,4},{12,8},{16,12},{20,16},{24,20},{28,24},{5,1},{9,5},{13... | collective-permute-start | bytes 1769480 | tf_op jit(solution)/shard_map/ppermute | solution.py:17
  182.4 46.7 %collective-permute-start.7 = (bf16[768,384]{1,0:T(8,128)(2,1)}, bf16[768,384]{1,0:T(8,128)(2,1)}, u32[]{:S(2)}, u32[]{:S(2)}) collective-permute-start(bf16[768,384]{1,0:T(8,128)(2,1)} %pad_maximum_fusion.6), channel_id=1, source_target_pairs={{0,4},{4,8},{8,12},{12,16},{16,20},{20,24},{24,28},{1,5},{5,9},{9,... | collective-permute-start | bytes 1769480 | tf_op jit(solution)/shard_map/ppermute | solution.py:17
  195.7 2.7 %copy-start = (bf16[3,384,2304]{1,2,0:T(8,128)(2,1)}, bf16[3,384,2304]{1,2,0:T(8,128)(2,1)S(1)}, u32[]{:S(2)}) copy-start(bf16[3,384,2304]{1,2,0:T(8,128)(2,1)S(1)} %multiply_convert_fusion.1) | copy-start | bytes 15925252
  195.7 3.9 %copy-start.1 = (f32[2304,3,128]{0,2,1:T(8,128)S(1)}, f32[2304,3,128]{0,2,1:T(8,128)}, u32[]{:S(2)}) copy-start(f32[2304,3,128]{0,2,1:T(8,128)} %fusion.21) | copy-start | bytes 10616836
  210.3 21.0 %collective-permute-start.4 = (bf16[768,384]{1,0:T(8,128)(2,1)}, bf16[768,384]{1,0:T(8,128)(2,1)}, u32[]{:S(2)}, u32[]{:S(2)}) collective-permute-start(bf16[768,384]{1,0:T(8,128)(2,1)} %pad_maximum_fusion.3), channel_id=1, source_target_pairs={{4,0},{8,4},{12,8},{16,12},{20,16},{24,20},{28,24},{5,1},{9,5},{13... | collective-permute-start | bytes 1769480 | tf_op jit(solution)/shard_map/ppermute | solution.py:17
  213.5 26.5 %collective-permute-start.5 = (bf16[768,384]{1,0:T(8,128)(2,1)}, bf16[768,384]{1,0:T(8,128)(2,1)}, u32[]{:S(2)}, u32[]{:S(2)}) collective-permute-start(bf16[768,384]{1,0:T(8,128)(2,1)} %pad_maximum_fusion.4), channel_id=1, source_target_pairs={{0,4},{4,8},{8,12},{12,16},{16,20},{20,24},{24,28},{1,5},{5,9},{9,... | collective-permute-start | bytes 1769480 | tf_op jit(solution)/shard_map/ppermute | solution.py:17
  223.2 3.6 %copy-start.2 = (f32[384,3,128]{0,2,1:T(8,128)S(1)}, f32[384,3,128]{0,2,1:T(8,128)}, u32[]{:S(2)}) copy-start(f32[384,3,128]{0,2,1:T(8,128)} %get-tuple-element.13) | copy-start | bytes 1769476
Sparse Core Ops, SparseCore 0:
  10.0 82.4 all-gather.4
  94.1 37.4 all-gather.2
where the time goes:
time: 250 us; the launch traced here: 249 us
  waiting for transfers between devices  95.2 us (38%)
  matrix products  49.2 us (20%)
  other arithmetic  36.7 us (15%)
  starting transfers between devices  27.8 us (11%)
  local copies, waits for them, and re-layouts  25.9 us (10%)
  between operations  14.3 us (6%)
    ppermute x8, waiting for transfers between devices, passed_along(): return lax.ppermute(block, axis, route)  51.1 us
    all_gather x1, waiting for transfers between devices, local(): full_grad = lax.all_gather(grad_out, 'head', axis=1, tiled=True)  39.1 us
    ppermute x8, starting transfers between devices, passed_along(): return lax.ppermute(block, axis, route)  27.7 us
    convert_element_type x2, other arithmetic, local(): (softmax_rows * (softmax_grad - row_inner)).astype(jnp.bfloat16)  16.2 us
    sub x2, matrix products, local(): weights = jnp.exp(scores - row_peak)  15.5 us
    dot_general x2, matrix products, local(): jnp.einsum('qhd,khd->hqk', grad_tile, value_block, preferred_element_type...  9.98 us
    add x6, local copies, waits for them, and re-layouts, local(): key_sums[slab_index][neighbour] + key_part[offset:offset + tile_size]  7.88 us
    unnamed x28, local copies, waits for them, and re-layouts  7.88 us
  transfers between devices with their start and end apart: 10, of which 6 were waited for; matrix products, arithmetic and copies ran while one was open for 24% of the time, Pallas kernels for 0%

commit v1 on v0

--- a/solution.py
+++ b/solution.py
@@ -3,6 +3,7 @@
 import jax.numpy as jnp
 from jax import lax
 from jax.sharding import PartitionSpec as P
+from jax.lax import axis_index, axis_size, ppermute
 
 HD = 128
 TILE_T = 6
@@ -29,7 +30,19 @@
     inverse_root = 1.0 / math.sqrt(HD)
     video_place = lax.axis_index("tm") % VT
     flags = (video_place > 0, video_place >= 0, video_place < VT - 1)
-    full_grad = lax.all_gather(grad_out, "head", axis=1, tiled=True)
+    n_axis = axis_size("head")
+    items = [(kk, (kk + 1) % n_axis) for kk in range(n_axis)]
+    xs_all = [(kk, (kk - 1) % n_axis) for kk in range(n_axis)]
+    a_next, vec_out = ([grad_out], [grad_out])
+    for _ in range(n_axis // 2):
+        current_block = ppermute(a_next[-1], "head", perm=items)
+        a_next.append(current_block)
+    for _ in tuple(range((n_axis - 1) // 2)):
+        r_now = ppermute(vec_out[-1], "head", xs_all)
+        vec_out.append(r_now)
+    e_next = jnp.concatenate([*a_next[::-1], *vec_out[1:]], 1)
+    t_next = axis_index("head")
+    full_grad = jnp.roll(e_next, (t_next - n_axis // 2) * grad_out.shape[1], 1)
     attn_sum = jnp.einsum(
         "td,hd->th",
         full_grad,

time: 250 us -> 219 us (0.88)
  waiting for transfers between devices: 95.2 us -> 42 us
  local copies, waits for them, and re-layouts: 25.9 us -> 42.5 us
  starting transfers between devices: 27.8 us -> 30.9 us
    all_gather x1 -> x0, waiting for transfers between devices: 39.1 us -> none  [local(): full_grad = lax.all_gather(grad_out, 'head', axis=1, tiled=True)]
    unnamed x28 -> x43, local copies, waits for them, and re-layouts: 7.88 us -> 22.7 us
    ppermute x8, waiting for transfers between devices: 51.1 us -> 41.3 us  [passed_along(): return lax.ppermute(block, axis, route)]
    all_gather x1, waiting for transfers between devices: 3.64 us -> 0.01 us  [local(): lax.all_gather(w_out, 'tm', axis=1, tiled=True)]
    ppermute x0 -> x3, starting transfers between devices: none -> 2.61 us  [the longest x1 1.72 us: local(): r_now = ppermute(vec_out[-1], 'head', xs_all)]
  transfers between devices with their start and end apart: 10 -> 12, of which waited for: 6 -> 4; matrix products, arithmetic and copies ran while one was open for 24% -> 37% of each run, Pallas kernels for 0% -> 0%
where the time goes in v1:
time: 219 us; the launch traced here: 218 us
  matrix products  51.6 us (24%)
  local copies, waits for them, and re-layouts  42.5 us (19%)
  waiting for transfers between devices  42 us (19%)
  other arithmetic  36.9 us (17%)
  starting transfers between devices  30.9 us (14%)
  between operations  14.3 us (7%)
    ppermute x8, waiting for transfers between devices, passed_along(): return lax.ppermute(block, axis, route)  41.3 us
    ppermute x8, starting transfers between devices, passed_along(): return lax.ppermute(block, axis, route)  28.2 us
    unnamed x43, local copies, waits for them, and re-layouts  22.7 us
    sub x2, matrix products, local(): weights = jnp.exp(scores - row_peak)  17.4 us
    convert_element_type x2, other arithmetic, local(): (softmax_rows * (softmax_grad - row_inner)).astype(jnp.bfloat16)  16.2 us
    dot_general x2, matrix products, local(): jnp.einsum('qhd,khd->hqk', grad_tile, value_block, preferred_element_type...  9.94 us
    add x6, local copies, waits for them, and re-layouts, local(): key_sums[slab_index][neighbour] + key_part[offset:offset + tile_size]  7.85 us
    dot_general x2, matrix products, local(): jnp.einsum('hqk,qhd->khd', softmax_low, grad_tile, preferred_element_type...  7.57 us
  transfers between devices with their start and end apart: 12, of which 4 were waited for; matrix products, arithmetic and copies ran while one was open for 37% of the time, Pallas kernels for 0%

profile of v1, /device:TPU:0, one launch (start us, length us, event | category | flops | bytes accessed | tf_op | source)
XLA Modules:
  0.0 218.1 jit_solution(11496503159226749578)
XLA Ops:
  11.1 5.9 %collective-permute-start = (bf16[768,384]{0,1:T(8,128)(2,1)S(1)}, bf16[768,384]{0,1:T(8,128)(2,1)}, u32[]{:S(2)}, u32[]{:S(2)}) collective-permute-start(bf16[768,384]{0,1:T(8,128)(2,1)S(1)} %copy.38), channel_id=1, source_target_pairs={{0,4},{4,8},{8,12},{12,16},{16,20},{20,24},{24,28},{1,5},{5,9},{9,... | collective-permute-start | bytes 1769480 | tf_op jit(solution)/shard_map/ppermute | solution.py:18
  19.6 5.5 %collective-permute-start.5 = (bf16[768,384]{0,1:T(8,128)(2,1)S(1)}, bf16[768,384]{0,1:T(8,128)(2,1)}, u32[]{:S(2)}, u32[]{:S(2)}) collective-permute-start(bf16[768,384]{0,1:T(8,128)(2,1)S(1)} %copy.44), channel_id=1, source_target_pairs={{0,4},{4,8},{8,12},{12,16},{16,20},{20,24},{24,28},{1,5},{5,9},{9,... | collective-permute-start | bytes 1769480 | tf_op jit(solution)/shard_map/ppermute | solution.py:18
  28.0 2.4 %collective-permute-done.1 = bf16[768,384]{0,1:T(8,128)(2,1)S(1)} collective-permute-done((bf16[768,384]{0,1:T(8,128)(2,1)S(1)}, bf16[768,384]{0,1:T(8,128)(2,1)S(1)}, u32[]{:S(2)}, u32[]{:S(2)}) %collective-permute-start.1) | collective-permute-done | bytes 589856 | tf_op jit(solution)/shard_map/ppermute | solution.py:18
  32.1 25.0 %collective-permute-done = bf16[768,384]{0,1:T(8,128)(2,1)} collective-permute-done((bf16[768,384]{0,1:T(8,128)(2,1)S(1)}, bf16[768,384]{0,1:T(8,128)(2,1)}, u32[]{:S(2)}, u32[]{:S(2)}) %collective-permute-start) | collective-permute-done | bytes 589856 | tf_op jit(solution)/shard_map/ppermute | solution.py:18
  59.0 8.6 %fusion.58 = (f32[3,384]{1,0:T(4,128)S(1)}, f32[3,384,2304]{1,2,0:T(8,128)}) fusion(pred[2304]{0:T(1024)(128)(4,1)S(1)} %pad_add_fusion, bf16[2304,3,128]{0,2,1:T(8,128)(2,1)S(1)} %bitcast.77, bf16[384,3,128]{0,2,1:T(8,128)(2,1)} %bitcast.93), kind=kOutput, calls=%fused_computation.92 | convolution fusion | flops 690096384 | bytes 12688128 | tf_op jit(solution)/shard_map/sub | solution.py:81
  67.7 4.9 %collective-permute-done.5 = bf16[768,384]{0,1:T(8,128)(2,1)} collective-permute-done((bf16[768,384]{0,1:T(8,128)(2,1)S(1)}, bf16[768,384]{0,1:T(8,128)(2,1)}, u32[]{:S(2)}, u32[]{:S(2)}) %collective-permute-start.5) | collective-permute-done | bytes 589856 | tf_op jit(solution)/shard_map/ppermute | solution.py:18
  72.6 2.6 %pad_maximum_fusion.1 = bf16[2304,384]{0,1:T(8,128)(2,1)} fusion(bf16[768,384]{0,1:T(8,128)(2,1)} %collective-permute-done.6, bf16[768,384]{0,1:T(8,128)(2,1)S(1)} %copy.44, bf16[768,384]{0,1:T(8,128)(2,1)} %collective-permute-done.5), kind=kLoop, calls=%fused_computation.37 | loop fusion | flops 5308416 | bytes 3538944 | tf_op jit(solution)/shard_map/concatenate | solution.py:66
  75.1 8.8 %fusion.59 = (f32[3,384]{1,0:T(4,128)S(1)}, f32[3,384,2304]{1,2,0:T(8,128)}) fusion(pred[2304]{0:T(1024)(128)(4,1)} %copy-done.9, bf16[2304,3,128]{0,2,1:T(8,128)(2,1)S(1)} %bitcast.78, bf16[384,3,128]{0,2,1:T(8,128)(2,1)} %bitcast.91), kind=kOutput, calls=%fused_computation.93 | convolution fusion | flops 690096384 | bytes 12688128 | tf_op jit(solution)/shard_map/sub | solution.py:81
  83.9 2.4 %constant_dynamic-update-slice_fusion.7 = bf16[768,6144]{1,0:T(8,128)(2,1)} fusion(bf16[768,768]{1,0:T(8,128)(2,1)} %collective-permute-done.3), kind=kLoop, calls=%fused_computation.83 | loop fusion | bytes 2359296
  86.4 2.5 %constant_dynamic-update-slice_fusion.6 = bf16[768,6144]{1,0:T(8,128)(2,1)} fusion(bf16[768,6144]{1,0:T(8,128)(2,1)} %constant_dynamic-update-slice_fusion.7, bf16[768,768]{1,0:T(8,128)(2,1)} %collective-permute-done.2), kind=kLoop, calls=%fused_computation.82 | loop fusion | bytes 2359296
  90.0 2.4 %constant_dynamic-update-slice_fusion.4 = bf16[768,6144]{1,0:T(8,128)(2,1)} fusion(bf16[768,6144]{1,0:T(8,128)(2,1)} %constant_dynamic-update-slice_fusion.5, bf16[768,768]{1,0:T(8,128)(2,1)} %collective-permute-done.4), kind=kLoop, calls=%fused_computation.80 | loop fusion | bytes 2359296
  92.4 2.4 %constant_dynamic-update-slice_fusion.3 = bf16[768,6144]{1,0:T(8,128)(2,1)} fusion(bf16[768,6144]{1,0:T(8,128)(2,1)} %constant_dynamic-update-slice_fusion.4, bf16[768,768]{1,0:T(8,128)(2,1)} %collective-permute-done.3), kind=kLoop, calls=%fused_computation.79 | loop fusion | bytes 2359296
  94.8 2.4 %constant_dynamic-update-slice_fusion.2 = bf16[768,6144]{1,0:T(8,128)(2,1)} fusion(bf16[768,6144]{1,0:T(8,128)(2,1)} %constant_dynamic-update-slice_fusion.3, bf16[768,768]{1,0:T(8,128)(2,1)} %collective-permute-done.2), kind=kLoop, calls=%fused_computation.78 | loop fusion | bytes 2359296
  98.3 2.4 %constant_dynamic-update-slice_fusion = bf16[768,6144]{1,0:T(8,128)(2,1)} fusion(bf16[768,6144]{1,0:T(8,128)(2,1)} %constant_dynamic-update-slice_fusion.1, bf16[768,768]{1,0:T(8,128)(2,1)} %collective-permute-done.4), kind=kLoop, calls=%fused_computation.76 | loop fusion | bytes 2359296 | tf_op jit(solution)/shard_map/jit(_roll_dynamic)/concatenate | solution.py:45
  100.7 5.6 %fusion.30 = bf16[768,384]{0,1:T(8,128)(2,1)S(1)} fusion(bf16[384,3072]{1,0:T(8,128)(2,1)} %all-gather.2.cloned.1.call-done, bf16[768,6144]{1,0:T(8,128)(2,1)} %constant_dynamic-update-slice_fusion, s32[]{:T(128)S(6)} %select_n.36), kind=kOutput, calls=%fused_computation.38 | convolution fusion | flops 1812234240 | bytes 7667716 | tf_op jit(solution)/shard_map/td,hd->th/dot_general | solution.py:46
  106.4 6.0 %fusion.27 = f32[2304,3,128]{0,2,1:T(8,128)S(1)} fusion(bf16[384,3,128]{0,2,1:T(8,128)(2,1)S(1)} %bitcast.107, f32[3,384,2304]{1,2,0:T(8,128)} %get-tuple-element.20, f32[3,384]{1,0:T(4,128)S(1)} %get-tuple-element.19), kind=kOutput, calls=%fused_computation.35 | convolution fusion | flops 684785664 | bytes 14455296 | tf_op jit(solution)/shard_map/hqk,qhd->khd/dot_general | solution.py:101
  113.9 5.0 %multiply_reduce_fusion = (f32[3,384]{1,0:T(4,128)S(1)}, f32[3,384,2304]{1,2,0:T(8,128)}) fusion(f32[3,384,2304]{1,2,0:T(8,128)S(1)} %bitcast.84, f32[3,384]{1,0:T(4,128)S(1)} %get-tuple-element.19, bf16[384,3,128]{0,2,1:T(8,128)(2,1)S(1)} %bitcast.108, bf16[2304,3,128]{0,2,1:T(8,128)(2,1)S(1)} %bitcast.89), kind=kOutput, calls=%fused_computation.11 | convolution fusion | flops 687438720 | bytes 23307264 | tf_op jit(solution)/shard_map/qhd,khd->hqk/dot_general | solution.py:84
  118.9 8.3 %multiply_convert_fusion = bf16[3,384,2304]{1,2,0:T(8,128)(2,1)S(1)} fusion(f32[3,384,2304]{1,2,0:T(8,128)} %get-tuple-element.22, f32[3,384]{1,0:T(4,128)S(1)} %get-tuple-element.21, f32[3,384,2304]{1,2,0:T(8,128)} %get-tuple-element.20, f32[3,384]{1,0:T(4,128)S(1)} %get-tuple-element.19), kind=kLoop, calls=%fused_computation.10 | loop fusion | flops 10616832 | bytes 26551296 | tf_op jit(solution)/shard_map/convert_element_type | solution.py:88
  129.1 3.4 %fusion.23 = f32[2304,3,128]{0,2,1:T(8,128)} fusion(bf16[3,384,2304]{1,2,0:T(8,128)(2,1)S(1)} %multiply_convert_fusion, bf16[384,3,128]{0,2,1:T(8,128)(2,1)S(1)} %bitcast.94), kind=kOutput, calls=%fused_computation.33 | convolution fusion | flops 680361984 | bytes 9142272 | tf_op jit(solution)/shard_map/hqk,qhd->khd/dot_general | solution.py:97
  134.1 4.9 %multiply_reduce_fusion.1 = (f32[3,384]{1,0:T(4,128)S(1)}, f32[3,384,2304]{1,2,0:T(8,128)}) fusion(f32[3,384,2304]{1,2,0:T(8,128)S(1)} %bitcast.82, f32[3,384]{1,0:T(4,128)S(1)} %get-tuple-element.23, bf16[384,3,128]{0,2,1:T(8,128)(2,1)S(1)} %bitcast.106, bf16[2304,3,128]{0,2,1:T(8,128)(2,1)S(1)} %bitcast.90), kind=kOutput, calls=%fused_computation.14 | convolution fusion | flops 687438720 | bytes 23307264 | tf_op jit(solution)/shard_map/qhd,khd->hqk/dot_general | solution.py:84
  148.1 1.9 pad_maximum_fusion.6
  150.1 6.0 %collective-permute-start.10 = (bf16[768,384]{1,0:T(8,128)(2,1)}, bf16[768,384]{1,0:T(8,128)(2,1)}, u32[]{:S(2)}, u32[]{:S(2)}) collective-permute-start(bf16[768,384]{1,0:T(8,128)(2,1)} %pad_maximum_fusion.6), channel_id=1, source_target_pairs={{0,4},{4,8},{8,12},{12,16},{16,20},{20,24},{24,28},{1,5},{5,9},{9,... | collective-permute-start | bytes 1769480 | tf_op jit(solution)/shard_map/ppermute | solution.py:18
  156.1 8.0 %multiply_convert_fusion.1 = bf16[3,384,2304]{1,2,0:T(8,128)(2,1)S(1)} fusion(f32[3,384,2304]{1,2,0:T(8,128)} %get-tuple-element.26, f32[3,384]{1,0:T(4,128)S(1)} %get-tuple-element.25, f32[3,384,2304]{1,2,0:T(8,128)} %get-tuple-element.24, f32[3,384]{1,0:T(4,128)S(1)} %get-tuple-element.23), kind=kLoop, calls=%fused_computation.13 | loop fusion | flops 10616832 | bytes 26551296 | tf_op jit(solution)/shard_map/convert_element_type | solution.py:88
  171.2 1.9 copy.69
  176.8 1.9 pad_maximum_fusion.3
  180.0 1.9 pad_maximum_fusion.4
  181.9 5.7 %collective-permute-start.8 = (bf16[768,384]{1,0:T(8,128)(2,1)}, bf16[768,384]{1,0:T(8,128)(2,1)}, u32[]{:S(2)}, u32[]{:S(2)}) collective-permute-start(bf16[768,384]{1,0:T(8,128)(2,1)} %pad_maximum_fusion.4), channel_id=1, source_target_pairs={{0,4},{4,8},{8,12},{12,16},{16,20},{20,24},{24,28},{1,5},{5,9},{9,... | collective-permute-start | bytes 1769480 | tf_op jit(solution)/shard_map/ppermute | solution.py:18
  187.6 4.3 %fusion.33 = bf16[3,128,384]{2,1,0:T(8,128)(2,1)} fusion(bf16[2304,3,128]{0,2,1:T(8,128)(2,1)S(1)} %bitcast.80, bf16[3,384,2304]{1,2,0:T(8,128)(2,1)} %copy-done), kind=kOutput, calls=%fused_computation.41 | convolution fusion | flops 679772160 | bytes 7372800 | tf_op jit(solution)/shard_map/hqk,khd->qhd/dot_general | solution.py:91
  191.9 1.9 copy.61
  197.8 2.2 %fusion.38 = bf16[768,384]{1,0:T(8,128)(2,1)} fusion(f32[384,384]{1,0:T(8,128)S(1)} %copy.73, f32[384,384]{1,0:T(8,128)S(1)} %copy.72, bf16[768,384]{1,0:T(8,128)(2,1)} %collective-permute-done.10, bf16[768,384]{1,0:T(8,128)(2,1)} %collective-permute-done.9), kind=kLoop, calls=%fused_computation.48 | loop fusion | flops 1769472 | bytes 2949120 | tf_op jit(solution)/shard_map/convert_element_type | solution.py:135
  200.1 8.9 %collective-permute-done.8 = bf16[768,384]{1,0:T(8,128)(2,1)} collective-permute-done((bf16[768,384]{1,0:T(8,128)(2,1)}, bf16[768,384]{1,0:T(8,128)(2,1)}, u32[]{:S(2)}, u32[]{:S(2)}) %collective-permute-start.8) | collective-permute-done | bytes 589856 | tf_op jit(solution)/shard_map/ppermute | solution.py:18
  209.0 2.2 %fusion.36 = bf16[768,384]{1,0:T(8,128)(2,1)} fusion(f32[384,384]{1,0:T(8,128)S(1)} %copy.65, f32[384,384]{1,0:T(8,128)S(1)} %copy.64, bf16[768,384]{1,0:T(8,128)(2,1)} %collective-permute-done.8, bf16[768,384]{1,0:T(8,128)(2,1)} %collective-permute-done.7), kind=kLoop, calls=%fused_computation.45 | loop fusion | flops 1769472 | bytes 2949120 | tf_op jit(solution)/shard_map/convert_element_type | solution.py:135
  (83 shorter events, 45.5 us)
Async XLA Ops:
  7.2 23.2 %copy-start.2 = (bf16[768,768]{1,0:T(8,128)(2,1)S(1)}, bf16[768,768]{1,0:T(8,128)(2,1)}, u32[]{:S(2)}) copy-start(bf16[768,768]{1,0:T(8,128)(2,1)} %param.8) | copy-start | bytes 3538948
  7.2 93.6 %all-gather.2.cloned.1.call-start = ((), (), s32[]{:S(2)}) async-start(), calls=%async_computation | async-start | bytes 2654208 | tf_op jit(solution)/shard_map/all_gather | solution.py:49
  7.9 50.8 %collective-permute-start.2 = (bf16[768,768]{1,0:T(8,128)(2,1)}, bf16[768,768]{1,0:T(8,128)(2,1)}, u32[]{:S(2)}, u32[]{:S(2)}) collective-permute-start(bf16[768,768]{1,0:T(8,128)(2,1)} %param.8), channel_id=1, source_target_pairs={{0,1},{1,2},{2,3},{3,0},{4,5},{5,6},{6,7},{7,4},{8,9},{9,10},{10,1... | collective-permute-start | bytes 3538952 | tf_op jit(solution)/shard_map/ppermute | solution.py:38
  9.8 22.4 %copy-start.4 = (bf16[768,384]{0,1:T(8,128)(2,1)}, bf16[768,384]{0,1:T(8,128)(2,1)S(1)}, u32[]{:S(2)}) copy-start(bf16[768,384]{0,1:T(8,128)(2,1)S(1)} %copy.38) | copy-start | bytes 1769476
  9.8 20.6 %collective-permute-start.1 = (bf16[768,384]{0,1:T(8,128)(2,1)S(1)}, bf16[768,384]{0,1:T(8,128)(2,1)S(1)}, u32[]{:S(2)}, u32[]{:S(2)}) collective-permute-start(bf16[768,384]{0,1:T(8,128)(2,1)S(1)} %copy.38), channel_id=1, source_target_pairs={{4,0},{8,4},{12,8},{16,12},{20,16},{24,20},{28,24},{5,1},{9,5},{13... | collective-permute-start | bytes 1769480 | tf_op jit(solution)/shard_map/ppermute | solution.py:18
  11.1 46.1 %collective-permute-start = (bf16[768,384]{0,1:T(8,128)(2,1)S(1)}, bf16[768,384]{0,1:T(8,128)(2,1)}, u32[]{:S(2)}, u32[]{:S(2)}) collective-permute-start(bf16[768,384]{0,1:T(8,128)(2,1)S(1)} %copy.38), channel_id=1, source_target_pairs={{0,4},{4,8},{8,12},{12,16},{16,20},{20,24},{24,28},{1,5},{5,9},{9,... | collective-permute-start | bytes 1769480 | tf_op jit(solution)/shard_map/ppermute | solution.py:18
  18.3 49.4 %collective-permute-start.6 = (bf16[768,384]{0,1:T(8,128)(2,1)S(1)}, bf16[768,384]{0,1:T(8,128)(2,1)}, u32[]{:S(2)}, u32[]{:S(2)}) collective-permute-start(bf16[768,384]{0,1:T(8,128)(2,1)S(1)} %copy.44), channel_id=1, source_target_pairs={{4,0},{8,4},{12,8},{16,12},{20,16},{24,20},{28,24},{5,1},{9,5},{13... | collective-permute-start | bytes 1769480 | tf_op jit(solution)/shard_map/ppermute | solution.py:18
  19.6 53.0 %collective-permute-start.5 = (bf16[768,384]{0,1:T(8,128)(2,1)S(1)}, bf16[768,384]{0,1:T(8,128)(2,1)}, u32[]{:S(2)}, u32[]{:S(2)}) collective-permute-start(bf16[768,384]{0,1:T(8,128)(2,1)S(1)} %copy.44), channel_id=1, source_target_pairs={{0,4},{4,8},{8,12},{12,16},{16,20},{20,24},{24,28},{1,5},{5,9},{9,... | collective-permute-start | bytes 1769480 | tf_op jit(solution)/shard_map/ppermute | solution.py:18
  28.0 39.7 %copy-start.9 = (pred[2304]{0:T(1024)(128)(4,1)}, pred[2304]{0:T(1024)(128)(4,1)S(1)}, u32[]{:S(2)}) copy-start(pred[2304]{0:T(1024)(128)(4,1)S(1)} %pad_add_fusion) | copy-start | bytes 6916
  30.4 1.7 copy-start.8
  30.4 59.6 %collective-permute-start.4 = (bf16[768,768]{1,0:T(8,128)(2,1)S(1)}, bf16[768,768]{1,0:T(8,128)(2,1)}, u32[]{:S(2)}, u32[]{:S(2)}) collective-permute-start(bf16[768,768]{1,0:T(8,128)(2,1)S(1)} %copy-done.2), channel_id=1, source_target_pairs={{0,3},{1,0},{2,1},{3,2},{4,7},{5,4},{6,5},{7,6},{8,11},{9,8},{10,9... | collective-permute-start | bytes 3538952 | tf_op jit(solution)/shard_map/ppermute | solution.py:41
  58.7 25.2 %collective-permute-start.3 = (bf16[768,768]{1,0:T(8,128)(2,1)}, bf16[768,768]{1,0:T(8,128)(2,1)}, u32[]{:S(2)}, u32[]{:S(2)}) collective-permute-start(bf16[768,768]{1,0:T(8,128)(2,1)} %collective-permute-done.2), channel_id=1, source_target_pairs={{0,1},{1,2},{2,3},{3,0},{4,5},{5,6},{6,7},{7,4},{8,9},{9,10},{10,1... | collective-permute-start | bytes 3538952 | tf_op jit(solution)/shard_map/ppermute | solution.py:38
  106.3 6.1 %slice-start.3 = ((s8[10616832]{0:T(1024)(128)(4,1)}), s8[4194304]{0:T(1024)(128)(4,1)S(1)}, s32[]{:S(2)}) async-start(s8[10616832]{0:T(1024)(128)(4,1)} %bitcast.83), calls=%async_computation.4 | async-start | bytes 8388608
  106.4 6.4 %slice-start.4 = ((s8[10616832]{0:T(1024)(128)(4,1)}), s8[4194304]{0:T(1024)(128)(4,1)S(1)}, s32[]{:S(2)}) async-start(s8[10616832]{0:T(1024)(128)(4,1)} %bitcast.83), calls=%async_computation.5 | async-start | bytes 8388608
  106.4 7.1 %slice-start.5 = ((s8[10616832]{0:T(1024)(128)(4,1)}), s8[2228224]{0:T(1024)(128)(4,1)S(1)}, s32[]{:S(2)}) async-start(s8[10616832]{0:T(1024)(128)(4,1)} %bitcast.83), calls=%async_computation.6 | async-start | bytes 4456448
  106.4 7.5 %copy-start.5 = (bf16[2304,384]{0,1:T(8,128)(2,1)S(1)}, bf16[2304,384]{0,1:T(8,128)(2,1)}, u32[]{:S(2)}) copy-start(bf16[2304,384]{0,1:T(8,128)(2,1)} %pad_maximum_fusion.1) | copy-start | bytes 5308420
  118.9 13.6 %slice-start = ((s8[10616832]{0:T(1024)(128)(4,1)}), s8[4194304]{0:T(1024)(128)(4,1)S(1)}, s32[]{:S(2)}) async-start(s8[10616832]{0:T(1024)(128)(4,1)} %bitcast.81), calls=%async_computation.1 | async-start | bytes 8388608
  118.9 13.6 %slice-start.1 = ((s8[10616832]{0:T(1024)(128)(4,1)}), s8[4194304]{0:T(1024)(128)(4,1)S(1)}, s32[]{:S(2)}) async-start(s8[10616832]{0:T(1024)(128)(4,1)} %bitcast.81), calls=%async_computation.2 | async-start | bytes 8388608
  127.2 1.9 copy-start.7
  127.2 5.2 %slice-start.2 = ((s8[10616832]{0:T(1024)(128)(4,1)}), s8[2228224]{0:T(1024)(128)(4,1)S(1)}, s32[]{:S(2)}) async-start(s8[10616832]{0:T(1024)(128)(4,1)} %bitcast.81), calls=%async_computation.3 | async-start | bytes 4456448
  146.8 51.0 %collective-permute-start.9 = (bf16[768,384]{1,0:T(8,128)(2,1)}, bf16[768,384]{1,0:T(8,128)(2,1)}, u32[]{:S(2)}, u32[]{:S(2)}) collective-permute-start(bf16[768,384]{1,0:T(8,128)(2,1)} %pad_maximum_fusion.5), channel_id=1, source_target_pairs={{4,0},{8,4},{12,8},{16,12},{20,16},{24,20},{28,24},{5,1},{9,5},{13... | collective-permute-start | bytes 1769480 | tf_op jit(solution)/shard_map/ppermute | solution.py:18
  150.1 47.7 %collective-permute-start.10 = (bf16[768,384]{1,0:T(8,128)(2,1)}, bf16[768,384]{1,0:T(8,128)(2,1)}, u32[]{:S(2)}, u32[]{:S(2)}) collective-permute-start(bf16[768,384]{1,0:T(8,128)(2,1)} %pad_maximum_fusion.6), channel_id=1, source_target_pairs={{0,4},{4,8},{8,12},{12,16},{16,20},{20,24},{24,28},{1,5},{5,9},{9,... | collective-permute-start | bytes 1769480 | tf_op jit(solution)/shard_map/ppermute | solution.py:18
  156.1 8.0 %copy-start.6 = (bf16[384,384]{0,1:T(8,128)(2,1)S(1)}, bf16[384,384]{0,1:T(8,128)(2,1)}, u32[]{:S(2)}) copy-start(bf16[384,384]{0,1:T(8,128)(2,1)} %copy.94) | copy-start | bytes 884740
  164.1 2.7 %copy-start = (bf16[3,384,2304]{1,2,0:T(8,128)(2,1)}, bf16[3,384,2304]{1,2,0:T(8,128)(2,1)S(1)}, u32[]{:S(2)}) copy-start(bf16[3,384,2304]{1,2,0:T(8,128)(2,1)S(1)} %multiply_convert_fusion.1) | copy-start | bytes 15925252
  164.1 3.9 %copy-start.1 = (f32[2304,3,128]{0,2,1:T(8,128)S(1)}, f32[2304,3,128]{0,2,1:T(8,128)}, u32[]{:S(2)}) copy-start(f32[2304,3,128]{0,2,1:T(8,128)} %fusion.23) | copy-start | bytes 10616836
  178.7 21.4 %collective-permute-start.7 = (bf16[768,384]{1,0:T(8,128)(2,1)}, bf16[768,384]{1,0:T(8,128)(2,1)}, u32[]{:S(2)}, u32[]{:S(2)}) collective-permute-start(bf16[768,384]{1,0:T(8,128)(2,1)} %pad_maximum_fusion.3), channel_id=1, source_target_pairs={{4,0},{8,4},{12,8},{16,12},{20,16},{24,20},{28,24},{5,1},{9,5},{13... | collective-permute-start | bytes 1769480 | tf_op jit(solution)/shard_map/ppermute | solution.py:18
  181.9 27.1 %collective-permute-start.8 = (bf16[768,384]{1,0:T(8,128)(2,1)}, bf16[768,384]{1,0:T(8,128)(2,1)}, u32[]{:S(2)}, u32[]{:S(2)}) collective-permute-start(bf16[768,384]{1,0:T(8,128)(2,1)} %pad_maximum_fusion.4), channel_id=1, source_target_pairs={{0,4},{4,8},{8,12},{12,16},{16,20},{20,24},{24,28},{1,5},{5,9},{9,... | collective-permute-start | bytes 1769480 | tf_op jit(solution)/shard_map/ppermute | solution.py:18
  191.9 3.6 %copy-start.3 = (f32[384,3,128]{0,2,1:T(8,128)S(1)}, f32[384,3,128]{0,2,1:T(8,128)}, u32[]{:S(2)}) copy-start(f32[384,3,128]{0,2,1:T(8,128)} %get-tuple-element.13) | copy-start | bytes 1769476
Sparse Core Ops, SparseCore 0:
  10.0 82.9 all-gather.1
